TPU v7x, 32 devices: a whole 2x2x4 slice. The times are simulated.
32 devices in a mesh: dp: 4 (over y, core), ctx: 4 (over z), tp: 2 (over x).
Axes of the slice: x: 2, y: 2, z: 4, core: 2. Of those that a mesh axis runs over, the one named last changes fastest.
Arguments:
- query_rows: bfloat16 [2048, 128, 128], P(('dp', 'ctx'), 'tp'), parts along dimension 0, may hold values from -6 to 6
- key_rows: bfloat16 [2048, 8, 128], P(('dp', 'ctx'), 'tp'), parts along dimension 0, may hold values from -6 to 6
- value_rows: bfloat16 [2048, 8, 128], P(('dp', 'ctx'), 'tp'), parts along dimension 0, may hold values from -6 to 6
- out_grad: bfloat16 [2048, 128, 128], P(('dp', 'ctx'), 'tp'), parts along dimension 0, may hold values from -6 to 6
- softmax_delta: float32 [2, 64, 2048], P('tp', 'ctx', 'dp'), parts along dimension 2, may hold values from -4 to 4
- log_norm: float32 [2, 64, 2048], P('tp', 'ctx', 'dp'), parts along dimension 2
- doc_lengths: int32 [12], P('dp'), parts along dimension 0, may hold values from 1 to 384, as said below
Outputs:
- query_grad: bfloat16 [2048, 128, 128], P(('dp', 'ctx'), 'tp'), parts along dimension 0
- key_grad: bfloat16 [2048, 8, 128], P(('dp', 'ctx'), 'tp'), parts along dimension 0
- value_grad: bfloat16 [2048, 8, 128], P(('dp', 'ctx'), 'tp'), parts along dimension 0
There are 4 independent parts, one for each index of `dp`. A program takes and returns all parts, laid end to end along the dimension named above; each array names one. Nothing has to cross between parts.
Inputs may be any that keep to these rules, and one draw needn't show every extreme that they name: `doc_lengths`: the 3 lengths sum to 512.
All inputs are finite; a program needn't handle non-finite values.
Results may differ from a plain program's by a relative error of at most 0.0056.
Values may be sent and summed in bfloat16 or wider, within the bound.
No kernel may reach another device: no remote copies, remote signals or barrier semaphores. Data moves between devices by JAX's collectives and lax.ppermute only.
A program may use at most 64 MiB of HBM per device.

v0:
```python
import functools

import jax
import jax.numpy as jnp
from jax import lax
from jax.experimental import pallas as pl
from jax.experimental.pallas import tpu as pltpu
from jax.sharding import PartitionSpec as P


DOC_MAX = 384
LOG2E = 1.4426950408889634
MIB = 1024 * 1024
VMEM = pl.BlockSpec(memory_space=pltpu.VMEM)
HBM = pl.BlockSpec(memory_space=pltpu.HBM)


def dot_nt(left, right):
    return lax.dot_general(left, right, (((1,), (1,)), ((), ())), preferred_element_type=jnp.float32)


def dot_nn(left, right):
    return lax.dot_general(left, right, (((1,), (0,)), ((), ())), preferred_element_type=jnp.float32)


def doc_start(docs_ref, token):
    start = jnp.zeros_like(token)
    end = jnp.int32(0)
    for d in range(docs_ref.shape[0]):
        end = end + docs_ref[d]
        start = jnp.where(token >= end, end, start)
    return start


def row_tokens(rows, share, first):
    return first + lax.broadcasted_iota(jnp.int32, (1, rows), 1) // share


def spread_stats(share, in_ref, out_ref):
    kv_heads, _, _, tok = in_ref.shape
    rows = tok * share
    x = in_ref[...].reshape(kv_heads * 2 * share, tok)
    high = x.astype(jnp.bfloat16)
    rest = x - high.astype(jnp.float32)
    mid = rest.astype(jnp.bfloat16)
    low = (rest - mid.astype(jnp.float32)).astype(jnp.bfloat16)
    at = lax.broadcasted_iota(jnp.int32, (tok, rows), 1) // share
    spread = (at == lax.broadcasted_iota(jnp.int32, (tok, rows), 0)).astype(jnp.float32)
    spread = spread.astype(jnp.bfloat16)
    parts = jnp.concatenate([high, mid, low], axis=1)
    y = dot_nn(parts, jnp.concatenate([spread] * 3, axis=0))
    own = lax.broadcasted_iota(jnp.int32, (share, rows), 1) % share
    own = own == lax.broadcasted_iota(jnp.int32, (share, rows), 0)
    for i in range(kv_heads):
        for j, factor in ((0, LOG2E), (1, 1.0)):
            first = (2 * i + j) * share
            row = jnp.sum(jnp.where(own, y[first : first + share], 0.0), axis=0, keepdims=True)
            out_ref[i, j : j + 1] = row * factor


def tile_grads(k, v, q, g, norm, delta, ok):
    scores = dot_nt(k, q)
    probs = jnp.exp2(scores * (q.shape[1] ** (-0.5) * LOG2E) - norm)
    if ok is not None:
        probs = jnp.where(ok, probs, 0.0)
    ds = (probs * (dot_nt(v, g) - delta)).astype(jnp.bfloat16)
    return ds, dot_nn(ds, q), dot_nn(probs.astype(jnp.bfloat16), g)


def head_rows(ref, i, share, first, count):
    block = ref[pl.ds(first, count), pl.ds(pl.multiple_of(i * share, share), share), :]
    return block.reshape(count * share, ref.shape[2])


def past_kernel(shift, share, lead, start_ref, q_ref, g_ref, stats_ref, kv_ref, ds_ref, outs, acc_ref, ready):
    tok, _, dim = q_ref.shape
    kv_heads, keys, _ = ds_ref.shape
    scaling = dim ** (-0.5)
    base = (lax.axis_index("ctx") - shift) * keys
    none = (base < 0) | (jnp.min(start_ref[...]) >= base + keys)
    full = jnp.logical_not(none) & (jnp.max(start_ref[...]) <= base)

    @pl.when(full)
    def _():
        for i in range(kv_heads):
            ready(i)
            q = head_rows(q_ref, lead + i, share, 0, tok)
            g = head_rows(g_ref, lead + i, share, 0, tok)
            ds, dk, dv = tile_grads(
                kv_ref[0, lead + i], kv_ref[1, lead + i], q, g, stats_ref[lead + i, 0:1], stats_ref[lead + i, 1:2], None
            )
            ds_ref[i] = ds
            out_ref = outs[i // outs[0].shape[1]]
            at = i % outs[0].shape[1]
            out_ref[0, at] = (dk * scaling).astype(out_ref.dtype)
            out_ref[1, at] = dv.astype(out_ref.dtype)

    @pl.when(jnp.logical_not(full))
    def _():
        for i in range(kv_heads):
            ready(i)

    @pl.when(none)
    def _():
        ds_ref[...] = jnp.zeros_like(ds_ref)
        for out_ref in outs:
            out_ref[...] = jnp.zeros_like(out_ref)

    @pl.when(jnp.logical_not(none | full))
    def _():
        step = 32

        def masked_head(out_ref, skip, i, _):
            acc_ref[...] = jnp.zeros_like(acc_ref)
            for b in range(tok // step):
                cut = slice(b * step * share, (b + 1) * step * share)
                start = start_ref[:, cut]
                reached = jnp.min(start) < base + keys

                @pl.when(reached)
                def _():
                    q = head_rows(q_ref, lead + i, share, b * step, step)
                    g = head_rows(g_ref, lead + i, share, b * step, step)
                    key = base + lax.broadcasted_iota(jnp.int32, (keys, step * share), 0)
                    ds, dk, dv = tile_grads(
                        kv_ref[0, lead + i],
                        kv_ref[1, lead + i],
                        q,
                        g,
                        stats_ref[lead + i, 0:1, cut],
                        stats_ref[lead + i, 1:2, cut],
                        key >= start,
                    )
                    ds_ref[i, :, cut] = ds
                    acc_ref[0] += dk
                    acc_ref[1] += dv

                @pl.when(jnp.logical_not(reached))
                def _():
                    ds_ref[i, :, cut] = jnp.zeros((keys, step * share), jnp.bfloat16)

            out_ref[0, i - skip] = (acc_ref[0] * scaling).astype(out_ref.dtype)
            out_ref[1, i - skip] = acc_ref[1].astype(out_ref.dtype)
            return 0

        for j, out_ref in enumerate(outs):
            skip = j * out_ref.shape[1]
            one_head = functools.partial(masked_head, out_ref, skip)
            lax.fori_loop(skip, skip + out_ref.shape[1], one_head, 0)


def first_past_kernel(share, docs_hbm, q_hbm, g_hbm, raw_ref, kv_ref, *refs):
    ds_ref, *outs = refs[:-9]
    q_ref, g_ref, stats_ref, start_ref, acc_ref, docs_ref, docs_sem, q_sem, g_sem = refs[-9:]
    tok = q_ref.shape[0]

    def copies(i):
        heads = pl.ds(i * share, share)
        return (
            pltpu.make_async_copy(q_hbm.at[:, heads, :], q_ref.at[:, heads, :], q_sem.at[i]),
            pltpu.make_async_copy(g_hbm.at[:, heads, :], g_ref.at[:, heads, :], g_sem.at[i]),
        )

    def ready(i):
        for copy in copies(i):
            copy.wait()

    docs_copy = pltpu.make_async_copy(docs_hbm, docs_ref, docs_sem)
    docs_copy.start()
    for i in range(kv_ref.shape[1]):
        for copy in copies(i):
            copy.start()
    spread_stats(share, raw_ref, stats_ref)
    docs_copy.wait()
    token = row_tokens(tok * share, share, lax.axis_index("ctx") * tok)
    start_ref[...] = doc_start(docs_ref, token)
    past_kernel(1, share, 0, start_ref, q_ref, g_ref, stats_ref, kv_ref, ds_ref, outs, acc_ref, ready)


def next_past_kernel(shift, share, lead, *refs):
    *ins, out_ref, acc_ref = refs
    past_kernel(shift, share, lead, *ins, [out_ref], acc_ref, lambda i: None)


def past_cost(kv_heads, keys, rows, dim):
    return pl.CostEstimate(
        flops=8 * kv_heads * keys * rows * dim,
        transcendentals=kv_heads * keys * rows,
        bytes_accessed=4 * kv_heads * rows * dim,
    )


def in_hbm(*arrays):
    return [pltpu.with_memory_space_constraint(x, pltpu.HBM) for x in arrays]


def first_past(share, halves, docs, q, g, raw, kv):
    _, kv_heads, keys, dim = kv.shape
    rows = q.shape[0] * share
    return pl.pallas_call(
        functools.partial(first_past_kernel, share),
        in_specs=[HBM, HBM, HBM, VMEM, VMEM],
        out_specs=[VMEM] * (5 + halves),
        out_shape=[
            jax.ShapeDtypeStruct((kv_heads, keys, rows), jnp.bfloat16),
        ]
        + [jax.ShapeDtypeStruct((2, kv_heads // halves, keys, dim), jnp.float32)] * halves
        + [
            jax.ShapeDtypeStruct(q.shape, q.dtype),
            jax.ShapeDtypeStruct(g.shape, g.dtype),
            jax.ShapeDtypeStruct((kv_heads, 2, rows), jnp.float32),
            jax.ShapeDtypeStruct((1, rows), jnp.int32),
        ],
        scratch_shapes=[
            pltpu.VMEM((2, keys, dim), jnp.float32),
            pltpu.SMEM(docs.shape, jnp.int32),
            pltpu.SemaphoreType.DMA,
            pltpu.SemaphoreType.DMA((kv_heads,)),
            pltpu.SemaphoreType.DMA((kv_heads,)),
        ],
        compiler_params=pltpu.CompilerParams(vmem_limit_bytes=32 * MIB),
        cost_estimate=past_cost(kv_heads, keys, rows, dim),
        name="past_1",
    )(*in_hbm(docs, q, g), raw, kv)


def next_past(shift, share, lead, kv_heads, start, q, g, stats, kv):
    _, _, keys, dim = kv.shape
    rows = stats.shape[2]
    return pl.pallas_call(
        functools.partial(next_past_kernel, shift, share, lead),
        in_specs=[VMEM] * 5,
        out_specs=[VMEM, VMEM],
        out_shape=[
            jax.ShapeDtypeStruct((kv_heads, keys, rows), jnp.bfloat16),
            jax.ShapeDtypeStruct((2, kv_heads, keys, dim), jnp.bfloat16),
        ],
        scratch_shapes=[pltpu.VMEM((2, keys, dim), jnp.float32)],
        compiler_params=pltpu.CompilerParams(vmem_limit_bytes=24 * MIB),
        cost_estimate=past_cost(kv_heads, keys, rows, dim),
    )(start, q, g, stats, kv)


def grouped(items, counts):
    groups, at = [], 0
    for count in counts:
        groups.append(items[at : at + count])
        at += count
    return groups


def own_kernel(share, start_ref, q_ref, g_ref, stats_ref, kv_ref, ds_ref, out_ref):
    tok, _, dim = q_ref.shape
    _, kv_heads, keys, _ = kv_ref.shape
    rows = tok * share
    scaling = dim ** (-0.5)
    first = lax.axis_index("ctx") * tok
    key = first + lax.broadcasted_iota(jnp.int32, (keys, rows), 0)
    ok = (key >= start_ref[...]) & (key <= row_tokens(rows, share, first))
    for i in range(kv_heads):
        q = head_rows(q_ref, i, share, 0, tok)
        g = head_rows(g_ref, i, share, 0, tok)
        ds, dk, dv = tile_grads(
            kv_ref[0, i], kv_ref[1, i], q, g, stats_ref[i, 0:1], stats_ref[i, 1:2], ok
        )
        ds_ref[i] = ds
        out_ref[0, i] = dk * scaling
        out_ref[1, i] = dv


def own_grads(share, start, q, g, stats, kv):
    _, kv_heads, keys, dim = kv.shape
    rows = stats.shape[2]
    return pl.pallas_call(
        functools.partial(own_kernel, share),
        in_specs=[VMEM] * 5,
        out_specs=[VMEM, VMEM],
        out_shape=[
            jax.ShapeDtypeStruct((kv_heads, keys, rows), jnp.bfloat16),
            jax.ShapeDtypeStruct(kv.shape, jnp.float32),
        ],
        compiler_params=pltpu.CompilerParams(vmem_limit_bytes=24 * MIB),
        cost_estimate=past_cost(kv_heads, keys, rows, dim),
        name="own",
    )(start, q, g, stats, kv)


def query_kernel(share, counts, *refs):
    n = len(counts)
    kvs, ds_refs, dq_ref = refs[:n], grouped(refs[n:-1], counts), refs[-1]
    tok, _, dim = dq_ref.shape
    scaling = dim ** (-0.5)
    for i in range(kvs[0].shape[1]):
        pieces = [r[i // r[0].shape[0]] for r in ds_refs]
        ks = jnp.concatenate([r[0, i] for r in kvs], axis=0)
        ds = jnp.concatenate([r[i % r.shape[0]] for r in pieces], axis=0)
        dq = dot_nn(ks.T, ds) * scaling
        dq_ref[:, i * share : (i + 1) * share, :] = dq.T.astype(jnp.bfloat16).reshape(tok, share, dim)


def query_grads(share, tok, kvs, ds_list):
    _, kv_heads, keys, dim = kvs[0].shape
    rows = tok * share
    n = len(kvs)
    counts = tuple(len(pieces) for pieces in ds_list)
    return pl.pallas_call(
        functools.partial(query_kernel, share, counts),
        in_specs=[VMEM] * (n + sum(counts)),
        out_specs=VMEM,
        out_shape=jax.ShapeDtypeStruct((tok, kv_heads * share, dim), jnp.bfloat16),
        compiler_params=pltpu.CompilerParams(vmem_limit_bytes=24 * MIB),
        cost_estimate=pl.CostEstimate(
            flops=2 * n * kv_heads * keys * rows * dim,
            transcendentals=0,
            bytes_accessed=2 * n * kv_heads * rows * dim,
        ),
        name="query",
    )(*kvs, *sum(ds_list, ()))


def sum_kernel(counts, *refs):
    own_ref, terms, (key_ref, value_ref) = refs[0], grouped(refs[1:-2], counts), refs[-2:]
    for j, ref in enumerate((key_ref, value_ref)):
        total = own_ref[j]
        for pieces in terms:
            term = jnp.concatenate([piece[j] for piece in pieces], axis=0)
            total = total + term.astype(jnp.float32)
        ref[...] = jnp.swapaxes(total.astype(jnp.bfloat16), 0, 1)


def sum_terms(own, terms):
    _, kv_heads, keys, dim = own.shape
    counts = tuple(len(pieces) for pieces in terms)
    return pl.pallas_call(
        functools.partial(sum_kernel, counts),
        in_specs=[VMEM] * (1 + sum(counts)),
        out_shape=[jax.ShapeDtypeStruct((keys, kv_heads, dim), jnp.bfloat16)] * 2,
        compiler_params=pltpu.CompilerParams(vmem_limit_bytes=24 * MIB),
        name="sum",
    )(own, *sum(terms, ()))


def local(query_rows, key_rows, value_rows, out_grad, softmax_delta, log_norm, doc_lengths):
    groups = lax.axis_size("ctx")
    tok, heads, _ = query_rows.shape
    kv_heads = key_rows.shape[1]
    share = heads // kv_heads
    per_dev = heads // groups
    reach = min(groups - 1, -(-(DOC_MAX - 1) // tok))

    def moved(x, s, first=0):
        pairs = [(i, i + s) for i in range(first, groups) if 0 <= i + s < groups]
        return lax.ppermute(x, "ctx", pairs)

    kvs = [jnp.stack([key_rows, value_rows]).transpose(0, 2, 1, 3)]
    for s in range(1, reach + 1):
        kvs.append(moved(kvs[1], 1, 1) if s == 2 else moved(kvs[0], s))
    raw = jnp.stack([log_norm[0], softmax_delta[0]])
    raw = raw.reshape(2, per_dev, groups, tok).transpose(2, 0, 1, 3)
    raw = lax.all_to_all(raw, "ctx", split_axis=0, concat_axis=0, tiled=True)
    raw = raw.reshape(kv_heads, groups // kv_heads, 2, per_dev, tok)
    raw = raw.transpose(0, 2, 1, 3, 4).reshape(kv_heads, 2, share, tok)
    halves = 2 if kv_heads % 2 == 0 else 1
    ds, *near, q, g, stats, start = first_past(
        share, halves, doc_lengths, query_rows, out_grad, raw, kvs[1]
    )
    part = kv_heads // halves
    ds_list, terms, hops = [(ds,)], [], []
    if reach >= 2:
        pieces = []
        for h in range(halves):
            ds, term = next_past(2, share, h * part, part, start, q, g, stats, kvs[2])
            pieces.append(ds)
            hops.append(moved(term, -1, 2))
        ds_list.append(tuple(pieces))
    for s in range(3, reach + 1):
        ds, term = next_past(s, share, 0, kv_heads, start, q, g, stats, kvs[s])
        ds_list.append((ds,))
        terms.append((moved(term, -s),))
    pieces = []
    for h in range(halves):
        term = near[h]
        if hops:
            term = term + hops[h].astype(jnp.float32)
        pieces.append(moved(term.astype(jnp.bfloat16), -1))
    terms.append(tuple(pieces))
    ds, total = own_grads(share, start, q, g, stats, kvs[0])
    ds_list.insert(0, (ds,))
    query_grad = query_grads(share, tok, kvs, ds_list)
    key_grad, value_grad = sum_terms(total, terms)
    return (query_grad, key_grad, value_grad)


def solution(mesh):
    rows = P(("dp", "ctx"), "tp", None)
    stats = P("tp", "ctx", "dp")
    return jax.shard_map(
        local,
        mesh=mesh,
        in_specs=(rows, rows, rows, rows, stats, stats, P("dp")),
        out_specs=(rows, rows, rows),
        check_vma=False,
    )
```

profile of v0, /device:TPU:0, one launch (start us, length us, event | category | flops | bytes accessed | tf_op | source)
XLA Modules:
  0.0 57.2 jit_solution(4757745588721178103)
XLA Ops:
  0.6 1.0 %copy_bitcast_fusion = (bf16[1,128,4,128]{3,1,2,0:T(8,128)(2,1)S(1)}, bf16[1,128,4,128]{3,1,2,0:T(8,128)(2,1)S(1)}) fusion(bf16[128,4,128]{2,1,0:T(4,128)(2,1)} %param.9, bf16[128,4,128]{2,1,0:T(4,128)(2,1)} %param.8), kind=kLoop, calls=%fused_computation.3 | loop fusion | bytes 524288 | tf_op jit(solution)/shard_map/stack | solution.py:355
  1.7 5.0 %collective-permute-start = (bf16[2,4,128,128]{3,2,1,0:T(8,128)(2,1)S(1)}, bf16[2,4,128,128]{3,2,1,0:T(8,128)(2,1)S(1)}, u32[]{:S(2)}, u32[]{:S(2)}) collective-permute-start(bf16[2,4,128,128]{3,2,1,0:T(8,128)(2,1)S(1)} %maximum_bitcast_fusion.kv_ref.refs_0_), channel_id=1, source_target_pairs={{0,2},{2,4},{4,6},{1,3},{3,5},{5,7},{8,10},{10,12},{12,14},{9,11},... | collective-permute-start | bytes 786440 | tf_op jit(solution)/shard_map/ppermute | solution.py:353
  6.7 3.3 %collective-permute-start.2 = (bf16[2,4,128,128]{3,2,1,0:T(8,128)(2,1)S(1)}, bf16[2,4,128,128]{3,2,1,0:T(8,128)(2,1)S(1)}, u32[]{:S(2)}, u32[]{:S(2)}) collective-permute-start(bf16[2,4,128,128]{3,2,1,0:T(8,128)(2,1)S(1)} %maximum_bitcast_fusion.kv_ref.refs_0_), channel_id=1, source_target_pairs={{0,6},{1,7},{8,14},{9,15},{16,22},{17,23},{24,30},{25,31}} | collective-permute-start | bytes 786440 | tf_op jit(solution)/shard_map/ppermute | solution.py:353
  10.0 3.3 %collective-permute-done.kv_ref.refs_1_ = bf16[2,4,128,128]{3,2,1,0:T(8,128)(2,1)S(1)} collective-permute-done((bf16[2,4,128,128]{3,2,1,0:T(8,128)(2,1)S(1)}, bf16[2,4,128,128]{3,2,1,0:T(8,128)(2,1)S(1)}, u32[]{:S(2)}, u32[]{:S(2)}) %collective-permute-start) | collective-permute-done | bytes 262176 | tf_op jit(solution)/shard_map/ppermute | solution.py:353
  13.3 0.7 %collective-permute-start.1 = (bf16[2,4,128,128]{3,2,1,0:T(8,128)(2,1)S(1)}, bf16[2,4,128,128]{3,2,1,0:T(8,128)(2,1)S(1)}, u32[]{:S(2)}, u32[]{:S(2)}) collective-permute-start(bf16[2,4,128,128]{3,2,1,0:T(8,128)(2,1)S(1)} %collective-permute-done.kv_ref.refs_1_), channel_id=1, source_target_pairs={{2,4},{4,6},{3,5},{5,7},{10,12},{12,14},{11,13},{13,15},{18,20},{2... | collective-permute-start | bytes 786440 | tf_op jit(solution)/shard_map/ppermute | solution.py:353
  14.0 0.8 %bitcast_bitcast_fusion = f32[4,2,16,128]{3,2,1,0:T(8,128)S(1)} fusion(f32[1,16,512]{2,1,0:T(8,128)} %param.11, f32[1,16,512]{2,1,0:T(8,128)} %param.12), kind=kLoop, calls=%fused_computation.5 | loop fusion | flops 16384 | bytes 131072 | tf_op jit(solution)/shard_map/transpose | solution.py:359
  14.8 17.7 %all_to_all.5.raw_ref = f32[4,2,16,128]{3,2,1,0:T(8,128)S(1)} all-to-all(f32[4,2,16,128]{3,2,1,0:T(8,128)S(1)} %bitcast_bitcast_fusion), channel_id=1, replica_groups=mesh['dp'=4,'ctx'=4,'tp'=2] {'ctx'}, dimensions={0} | all-to-all | bytes 131072 | tf_op jit(solution)/shard_map/all_to_all | solution.py:360
  32.5 2.5 %past_1.1 = (bf16[4,128,2048]{2,1,0:T(8,128)(2,1)S(1)}, f32[2,2,128,128]{3,2,1,0:T(8,128)S(1)}, f32[2,2,128,128]{3,2,1,0:T(8,128)S(1)}, bf16[128,64,128]{2,1,0:T...) custom-call(s32[3]{0:T(128)} %docs_hbm.1, ...), custom_call_target="tpu_custom_call" | custom-call | flops 1073741824 | bytes 4194304 | tf_op jit(solution)/shard_map/past_1/pallas_call | solution.py:200
  35.0 0.0 collective-permute-done.1.refs_4_.refs_2_
  35.0 0.3 shard_map.95
  35.3 0.7 %collective-permute-start.6 = (bf16[2,2,128,128]{3,2,1,0:T(8,128)(2,1)S(1)}, bf16[2,2,128,128]{3,2,1,0:T(8,128)(2,1)S(1)}, u32[]{:S(2)}, u32[]{:S(2)}) collective-permute-start(bf16[2,2,128,128]{3,2,1,0:T(8,128)(2,1)S(1)} %get-tuple-element.34), channel_id=1, source_target_pairs={{4,2},{6,4},{5,3},{7,5},{12,10},{14,12},{13,11},{15,13},{20,18},{2... | collective-permute-start | bytes 393224 | tf_op jit(solution)/shard_map/ppermute | solution.py:353
  36.0 0.0 collective-permute-done.2.refs_4_.refs_3_
  36.0 0.6 %shard_map.96 = (bf16[4,128,2048]{2,1,0:T(8,128)(2,1)S(1)}, bf16[2,4,128,128]{3,2,1,0:T(8,128)(2,1)S(1)}) custom-call(s32[1,2048]{1,0:T(1,128)S(1)} %get-tuple-element.20.start_ref.refs_0_, bf16[128,64,128]{2,1,0:T(8,128)(2,1)S(1)} %get-tuple-element.21.q_ref.refs_1_, bf16[128,64,128]{2,1,0:T(8,128)(2,1)S(1)} %get-tuple-element.22.g_ref.refs_2_, ...), custom_call_target="tpu_custom_call" | custom-call | flops 1073741824 | bytes 4194304 | tf_op jit(solution)/shard_map/pallas_call | solution.py:230
  36.6 1.3 %collective-permute-start.3 = (bf16[2,4,128,128]{3,2,1,0:T(8,128)(2,1)S(1)}, bf16[2,4,128,128]{3,2,1,0:T(8,128)(2,1)S(1)}, u32[]{:S(2)}, u32[]{:S(2)}) collective-permute-start(bf16[2,4,128,128]{3,2,1,0:T(8,128)(2,1)S(1)} %get-tuple-element.30), channel_id=1, source_target_pairs={{6,0},{7,1},{14,8},{15,9},{22,16},{23,17},{30,24},{31,25}} | collective-permute-start | bytes 786440 | tf_op jit(solution)/shard_map/ppermute | solution.py:353
  37.9 0.3 shard_map.94
  38.2 0.7 %collective-permute-start.4 = (bf16[2,2,128,128]{3,2,1,0:T(8,128)(2,1)S(1)}, bf16[2,2,128,128]{3,2,1,0:T(8,128)(2,1)S(1)}, u32[]{:S(2)}, u32[]{:S(2)}) collective-permute-start(bf16[2,2,128,128]{3,2,1,0:T(8,128)(2,1)S(1)} %get-tuple-element.32), channel_id=1, source_target_pairs={{4,2},{6,4},{5,3},{7,5},{12,10},{14,12},{13,11},{15,13},{20,18},{2... | collective-permute-start | bytes 393224 | tf_op jit(solution)/shard_map/ppermute | solution.py:353
  38.8 0.0 collective-permute-done.6
  38.9 1.3 %collective-permute-start.7 = (bf16[2,2,128,128]{3,2,1,0:T(8,128)(2,1)S(1)}, bf16[2,2,128,128]{3,2,1,0:T(8,128)(2,1)S(1)}, u32[]{:S(2)}, u32[]{:S(2)}) collective-permute-start(bf16[2,2,128,128]{3,2,1,0:T(8,128)(2,1)S(1)} %add_convert_fusion), channel_id=1, source_target_pairs={{2,0},{4,2},{6,4},{3,1},{5,3},{7,5},{10,8},{12,10},{14,12},{11,9},... | collective-permute-start | bytes 393224 | tf_op jit(solution)/shard_map/ppermute | solution.py:353
  40.2 0.0 collective-permute-done.4
  40.2 1.3 %collective-permute-start.5 = (bf16[2,2,128,128]{3,2,1,0:T(8,128)(2,1)S(1)}, bf16[2,2,128,128]{3,2,1,0:T(8,128)(2,1)S(1)}, u32[]{:S(2)}, u32[]{:S(2)}) collective-permute-start(bf16[2,2,128,128]{3,2,1,0:T(8,128)(2,1)S(1)} %add_convert_fusion.1), channel_id=1, source_target_pairs={{2,0},{4,2},{6,4},{3,1},{5,3},{7,5},{10,8},{12,10},{14,12},{11,9},... | collective-permute-start | bytes 393224 | tf_op jit(solution)/shard_map/ppermute | solution.py:353
  41.5 2.7 %own.1 = (bf16[4,128,2048]{2,1,0:T(8,128)(2,1)S(1)}, f32[2,4,128,128]{3,2,1,0:T(8,128)S(1)}) custom-call(s32[1,2048]{1,0:T(1,128)S(1)} %get-tuple-element.20.start_ref.refs_0_, bf16[128,64,128]{2,1,0:T(8,128)(2,1)S(1)} %get-tuple-element.21.q_ref.refs_1_, bf16[128,64,128]{2,1,0:T(8,128)(2,1)S(1)} %get-tuple-element.22.g_ref.refs_2_, ...), custom_call_target="tpu_custom_call" | custom-call | flops 1073741824 | bytes 4194304 | tf_op jit(solution)/shard_map/own/pallas_call | solution.py:274
  44.3 2.7 %query.1 = bf16[128,64,128]{2,1,0:T(8,128)(2,1)} custom-call(bf16[2,4,128,128]{3,2,1,0:T(8,128)(2,1)S(1)} %maximum_bitcast_fusion.kv_ref.refs_0_, bf16[2,4,128,128]{3,2,1,0:T(8,128)(2,1)S(1)} %collective-permute-done.kv_ref.refs_1_, bf16[2,4,128,128]{3,2,1,0:T(8,128)(2,1)S(1)} %collective-permute-done.1.refs_4_.refs_2_, ...), custom_call_target="tpu_custom_call" | custom-call | flops 1073741824 | bytes 8388608 | tf_op jit(solution)/shard_map/query/pallas_call | solution.py:306
  46.9 2.8 %collective-permute-done.3.refs_1_ = bf16[2,4,128,128]{3,2,1,0:T(8,128)(2,1)S(1)} collective-permute-done((bf16[2,4,128,128]{3,2,1,0:T(8,128)(2,1)S(1)}, bf16[2,4,128,128]{3,2,1,0:T(8,128)(2,1)S(1)}, u32[]{:S(2)}, u32[]{:S(2)}) %collective-permute-start.3) | collective-permute-done | bytes 262176 | tf_op jit(solution)/shard_map/ppermute | solution.py:353
  49.8 1.3 %collective-permute-done.7.refs_3_ = bf16[2,2,128,128]{3,2,1,0:T(8,128)(2,1)S(1)} collective-permute-done((bf16[2,2,128,128]{3,2,1,0:T(8,128)(2,1)S(1)}, bf16[2,2,128,128]{3,2,1,0:T(8,128)(2,1)S(1)}, u32[]{:S(2)}, u32[]{:S(2)}) %collective-permute-start.7) | collective-permute-done | bytes 131104 | tf_op jit(solution)/shard_map/ppermute | solution.py:353
  51.1 5.3 %collective-permute-done.5.refs_2_ = bf16[2,2,128,128]{3,2,1,0:T(8,128)(2,1)S(1)} collective-permute-done((bf16[2,2,128,128]{3,2,1,0:T(8,128)(2,1)S(1)}, bf16[2,2,128,128]{3,2,1,0:T(8,128)(2,1)S(1)}, u32[]{:S(2)}, u32[]{:S(2)}) %collective-permute-start.5) | collective-permute-done | bytes 131104 | tf_op jit(solution)/shard_map/ppermute | solution.py:353
  56.4 0.7 %sum.1 = (bf16[128,4,128]{2,1,0:T(4,128)(2,1)}, bf16[128,4,128]{2,1,0:T(4,128)(2,1)}) custom-call(f32[2,4,128,128]{3,2,1,0:T(8,128)S(1)} %get-tuple-element.29.refs_0_, bf16[2,4,128,128]{3,2,1,0:T(8,128)(2,1)S(1)} %collective-permute-done.3.refs_1_, bf16[2,2,128,128]{3,2,1,0:T(8,128)(2,1)S(1)} %collective-permute-done.5.refs_2_, ...), custom_call_target="tpu_custom_call" | custom-call | tf_op jit(solution)/shard_map/sum/pallas_call | solution.py:334
  (3 shorter events, 0.1 us)
Async XLA Ops:
  1.7 11.6 %collective-permute-start = (bf16[2,4,128,128]{3,2,1,0:T(8,128)(2,1)S(1)}, bf16[2,4,128,128]{3,2,1,0:T(8,128)(2,1)S(1)}, u32[]{:S(2)}, u32[]{:S(2)}) collective-permute-start(bf16[2,4,128,128]{3,2,1,0:T(8,128)(2,1)S(1)} %maximum_bitcast_fusion.kv_ref.refs_0_), channel_id=1, source_target_pairs={{0,2},{2,4},{4,6},{1,3},{3,5},{5,7},{8,10},{10,12},{12,14},{9,11},... | collective-permute-start | bytes 786440 | tf_op jit(solution)/shard_map/ppermute | solution.py:353
  6.7 29.3 %collective-permute-start.2 = (bf16[2,4,128,128]{3,2,1,0:T(8,128)(2,1)S(1)}, bf16[2,4,128,128]{3,2,1,0:T(8,128)(2,1)S(1)}, u32[]{:S(2)}, u32[]{:S(2)}) collective-permute-start(bf16[2,4,128,128]{3,2,1,0:T(8,128)(2,1)S(1)} %maximum_bitcast_fusion.kv_ref.refs_0_), channel_id=1, source_target_pairs={{0,6},{1,7},{8,14},{9,15},{16,22},{17,23},{24,30},{25,31}} | collective-permute-start | bytes 786440 | tf_op jit(solution)/shard_map/ppermute | solution.py:353
  13.3 21.6 %collective-permute-start.1 = (bf16[2,4,128,128]{3,2,1,0:T(8,128)(2,1)S(1)}, bf16[2,4,128,128]{3,2,1,0:T(8,128)(2,1)S(1)}, u32[]{:S(2)}, u32[]{:S(2)}) collective-permute-start(bf16[2,4,128,128]{3,2,1,0:T(8,128)(2,1)S(1)} %collective-permute-done.kv_ref.refs_1_), channel_id=1, source_target_pairs={{2,4},{4,6},{3,5},{5,7},{10,12},{12,14},{11,13},{13,15},{18,20},{2... | collective-permute-start | bytes 786440 | tf_op jit(solution)/shard_map/ppermute | solution.py:353
  35.3 3.6 %collective-permute-start.6 = (bf16[2,2,128,128]{3,2,1,0:T(8,128)(2,1)S(1)}, bf16[2,2,128,128]{3,2,1,0:T(8,128)(2,1)S(1)}, u32[]{:S(2)}, u32[]{:S(2)}) collective-permute-start(bf16[2,2,128,128]{3,2,1,0:T(8,128)(2,1)S(1)} %get-tuple-element.34), channel_id=1, source_target_pairs={{4,2},{6,4},{5,3},{7,5},{12,10},{14,12},{13,11},{15,13},{20,18},{2... | collective-permute-start | bytes 393224 | tf_op jit(solution)/shard_map/ppermute | solution.py:353
  36.6 13.2 %collective-permute-start.3 = (bf16[2,4,128,128]{3,2,1,0:T(8,128)(2,1)S(1)}, bf16[2,4,128,128]{3,2,1,0:T(8,128)(2,1)S(1)}, u32[]{:S(2)}, u32[]{:S(2)}) collective-permute-start(bf16[2,4,128,128]{3,2,1,0:T(8,128)(2,1)S(1)} %get-tuple-element.30), channel_id=1, source_target_pairs={{6,0},{7,1},{14,8},{15,9},{22,16},{23,17},{30,24},{31,25}} | collective-permute-start | bytes 786440 | tf_op jit(solution)/shard_map/ppermute | solution.py:353
  38.2 2.0 %collective-permute-start.4 = (bf16[2,2,128,128]{3,2,1,0:T(8,128)(2,1)S(1)}, bf16[2,2,128,128]{3,2,1,0:T(8,128)(2,1)S(1)}, u32[]{:S(2)}, u32[]{:S(2)}) collective-permute-start(bf16[2,2,128,128]{3,2,1,0:T(8,128)(2,1)S(1)} %get-tuple-element.32), channel_id=1, source_target_pairs={{4,2},{6,4},{5,3},{7,5},{12,10},{14,12},{13,11},{15,13},{20,18},{2... | collective-permute-start | bytes 393224 | tf_op jit(solution)/shard_map/ppermute | solution.py:353
  38.9 12.2 %collective-permute-start.7 = (bf16[2,2,128,128]{3,2,1,0:T(8,128)(2,1)S(1)}, bf16[2,2,128,128]{3,2,1,0:T(8,128)(2,1)S(1)}, u32[]{:S(2)}, u32[]{:S(2)}) collective-permute-start(bf16[2,2,128,128]{3,2,1,0:T(8,128)(2,1)S(1)} %add_convert_fusion), channel_id=1, source_target_pairs={{2,0},{4,2},{6,4},{3,1},{5,3},{7,5},{10,8},{12,10},{14,12},{11,9},... | collective-permute-start | bytes 393224 | tf_op jit(solution)/shard_map/ppermute | solution.py:353
  40.2 16.2 %collective-permute-start.5 = (bf16[2,2,128,128]{3,2,1,0:T(8,128)(2,1)S(1)}, bf16[2,2,128,128]{3,2,1,0:T(8,128)(2,1)S(1)}, u32[]{:S(2)}, u32[]{:S(2)}) collective-permute-start(bf16[2,2,128,128]{3,2,1,0:T(8,128)(2,1)S(1)} %add_convert_fusion.1), channel_id=1, source_target_pairs={{2,0},{4,2},{6,4},{3,1},{5,3},{7,5},{10,8},{12,10},{14,12},{11,9},... | collective-permute-start | bytes 393224 | tf_op jit(solution)/shard_map/ppermute | solution.py:353
where the time goes:
time: 57.6 us; the launch traced here: 57.2 us
  blocking collectives  17.7 us (31%)
  starting transfers between devices  14.2 us (25%)
  waiting for transfers between devices  12.8 us (22%)
  Pallas kernels  9.79 us (17%)
  local copies, waits for them, and re-layouts  1 us (2%)
  other arithmetic  0.87 us (2%)
  between operations  0.79 us (1%)
    all_to_all x1, blocking collectives, local(): raw = lax.all_to_all(raw, 'ctx', split_axis=0, concat_axis=0, tiled=True)  17.7 us
    ppermute x8, starting transfers between devices, moved(): return lax.ppermute(x, 'ctx', pairs)  14.2 us
    ppermute x8, waiting for transfers between devices, moved(): return lax.ppermute(x, 'ctx', pairs)  12.8 us
    pallas_call x1, Pallas kernels, own_grads(): pl.pallas_call(functools.partial(own_kernel, share), in_specs=[VMEM] * 5,...  2.7 us
    pallas_call x1, Pallas kernels, query_grads(): pl.pallas_call(functools.partial(query_kernel, share, counts), in_specs=[...  2.69 us
    pallas_call x1, Pallas kernels, first_past(): pl.pallas_call(functools.partial(first_past_kernel, share), in_specs=[HBM...  2.46 us
    pallas_call x3, Pallas kernels, next_past(): pl.pallas_call(functools.partial(next_past_kernel, shift, share, lead), i...  1.19 us
  transfers between devices with their start and end apart: 8, of which 4 were waited for; matrix products, arithmetic and copies ran while one was open for 1% of the time, Pallas kernels for 16%

commit v1 on v0

--- a/solution.py
+++ b/solution.py
@@ -249,7 +249,9 @@
     return groups
 
 
-def own_kernel(share, start_ref, q_ref, g_ref, stats_ref, kv_ref, ds_ref, out_ref):
+def last_kernel(share, counts, start_ref, q_ref, g_ref, stats_ref, kv_ref, *refs):
+    n = len(counts)
+    past_kv, past_ds, (dq_ref, out_ref) = refs[:n], grouped(refs[n:-2], counts), refs[-2:]
     tok, _, dim = q_ref.shape
     _, kv_heads, keys, _ = kv_ref.shape
     rows = tok * share
@@ -258,64 +260,40 @@
     key = first + lax.broadcasted_iota(jnp.int32, (keys, rows), 0)
     ok = (key >= start_ref[...]) & (key <= row_tokens(rows, share, first))
     for i in range(kv_heads):
+        k = kv_ref[0, i]
         q = head_rows(q_ref, i, share, 0, tok)
         g = head_rows(g_ref, i, share, 0, tok)
-        ds, dk, dv = tile_grads(
-            kv_ref[0, i], kv_ref[1, i], q, g, stats_ref[i, 0:1], stats_ref[i, 1:2], ok
-        )
-        ds_ref[i] = ds
+        ds, dk, dv = tile_grads(k, kv_ref[1, i], q, g, stats_ref[i, 0:1], stats_ref[i, 1:2], ok)
         out_ref[0, i] = dk * scaling
         out_ref[1, i] = dv
-
-
-def own_grads(share, start, q, g, stats, kv):
-    _, kv_heads, keys, dim = kv.shape
-    rows = stats.shape[2]
-    return pl.pallas_call(
-        functools.partial(own_kernel, share),
-        in_specs=[VMEM] * 5,
-        out_specs=[VMEM, VMEM],
-        out_shape=[
-            jax.ShapeDtypeStruct((kv_heads, keys, rows), jnp.bfloat16),
-            jax.ShapeDtypeStruct(kv.shape, jnp.float32),
-        ],
-        compiler_params=pltpu.CompilerParams(vmem_limit_bytes=24 * MIB),
-        cost_estimate=past_cost(kv_heads, keys, rows, dim),
-        name="own",
-    )(start, q, g, stats, kv)
-
-
-def query_kernel(share, counts, *refs):
-    n = len(counts)
-    kvs, ds_refs, dq_ref = refs[:n], grouped(refs[n:-1], counts), refs[-1]
-    tok, _, dim = dq_ref.shape
-    scaling = dim ** (-0.5)
-    for i in range(kvs[0].shape[1]):
-        pieces = [r[i // r[0].shape[0]] for r in ds_refs]
-        ks = jnp.concatenate([r[0, i] for r in kvs], axis=0)
-        ds = jnp.concatenate([r[i % r.shape[0]] for r in pieces], axis=0)
+        ks = jnp.concatenate([k] + [r[0, i] for r in past_kv], axis=0)
+        pieces = [r[i // r[0].shape[0]] for r in past_ds]
+        ds = jnp.concatenate([ds] + [r[i % r.shape[0]] for r in pieces], axis=0)
         dq = dot_nn(ks.T, ds) * scaling
         dq_ref[:, i * share : (i + 1) * share, :] = dq.T.astype(jnp.bfloat16).reshape(tok, share, dim)
 
 
-def query_grads(share, tok, kvs, ds_list):
+def last_grads(share, start, q, g, stats, kvs, ds_list):
     _, kv_heads, keys, dim = kvs[0].shape
-    rows = tok * share
+    rows = stats.shape[2]
     n = len(kvs)
     counts = tuple(len(pieces) for pieces in ds_list)
     return pl.pallas_call(
-        functools.partial(query_kernel, share, counts),
-        in_specs=[VMEM] * (n + sum(counts)),
-        out_specs=VMEM,
-        out_shape=jax.ShapeDtypeStruct((tok, kv_heads * share, dim), jnp.bfloat16),
+        functools.partial(last_kernel, share, counts),
+        in_specs=[VMEM] * (4 + n + sum(counts)),
+        out_specs=[VMEM, VMEM],
+        out_shape=[
+            jax.ShapeDtypeStruct(q.shape, jnp.bfloat16),
+            jax.ShapeDtypeStruct(kvs[0].shape, jnp.float32),
+        ],
         compiler_params=pltpu.CompilerParams(vmem_limit_bytes=24 * MIB),
         cost_estimate=pl.CostEstimate(
-            flops=2 * n * kv_heads * keys * rows * dim,
-            transcendentals=0,
-            bytes_accessed=2 * n * kv_heads * rows * dim,
+            flops=(8 + 2 * n) * kv_heads * keys * rows * dim,
+            transcendentals=kv_heads * keys * rows,
+            bytes_accessed=4 * kv_heads * rows * dim,
         ),
-        name="query",
-    )(*kvs, *sum(ds_list, ()))
+        name="last",
+    )(start, q, g, stats, *kvs, *sum(ds_list, ()))
 
 
 def sum_kernel(counts, *refs):
@@ -384,9 +362,7 @@
             term = term + hops[h].astype(jnp.float32)
         pieces.append(moved(term.astype(jnp.bfloat16), -1))
     terms.append(tuple(pieces))
-    ds, total = own_grads(share, start, q, g, stats, kvs[0])
-    ds_list.insert(0, (ds,))
-    query_grad = query_grads(share, tok, kvs, ds_list)
+    query_grad, total = last_grads(share, start, q, g, stats, kvs, ds_list)
     key_grad, value_grad = sum_terms(total, terms)
     return (query_grad, key_grad, value_grad)
 

time: 57.6 us -> 57.8 us (level)
    pallas_call x2 -> x1, Pallas kernels: 5.39 us -> 5.49 us  [last_grads(): pl.pallas_call(functools.partial(last_kernel, share, counts), in_specs=[V...]
where the time goes in v1:
time: 57.8 us; the launch traced here: 57.5 us
  blocking collectives  17.7 us (31%)
  starting transfers between devices  14.2 us (25%)
  waiting for transfers between devices  13 us (22%)
  Pallas kernels  9.9 us (17%)
  local copies, waits for them, and re-layouts  1 us (2%)
  other arithmetic  0.88 us (2%)
  between operations  0.78 us (1%)
    all_to_all x1, blocking collectives, local(): raw = lax.all_to_all(raw, 'ctx', split_axis=0, concat_axis=0, tiled=True)  17.7 us
    ppermute x8, starting transfers between devices, moved(): return lax.ppermute(x, 'ctx', pairs)  14.2 us
    ppermute x8, waiting for transfers between devices, moved(): return lax.ppermute(x, 'ctx', pairs)  13 us
    pallas_call x1, Pallas kernels, last_grads(): pl.pallas_call(functools.partial(last_kernel, share, counts), in_specs=[V...  5.49 us
    pallas_call x1, Pallas kernels, first_past(): pl.pallas_call(functools.partial(first_past_kernel, share), in_specs=[HBM...  2.46 us
    pallas_call x3, Pallas kernels, next_past(): pl.pallas_call(functools.partial(next_past_kernel, shift, share, lead), i...  1.19 us
  transfers between devices with their start and end apart: 8, of which 4 were waited for; matrix products, arithmetic and copies ran while one was open for 1% of the time, Pallas kernels for 16%

profile of v1, /device:TPU:0, one launch (start us, length us, event | category | flops | bytes accessed | tf_op | source)
XLA Modules:
  0.0 57.5 jit_solution(6238667175541506668)
XLA Ops:
  0.6 1.0 %copy_bitcast_fusion = (bf16[1,128,4,128]{3,1,2,0:T(8,128)(2,1)S(1)}, bf16[1,128,4,128]{3,1,2,0:T(8,128)(2,1)S(1)}) fusion(bf16[128,4,128]{2,1,0:T(4,128)(2,1)} %param.9, bf16[128,4,128]{2,1,0:T(4,128)(2,1)} %param.8), kind=kLoop, calls=%fused_computation.3 | loop fusion | bytes 524288 | tf_op jit(solution)/shard_map/stack | solution.py:333
  1.7 5.0 %collective-permute-start = (bf16[2,4,128,128]{3,2,1,0:T(8,128)(2,1)S(1)}, bf16[2,4,128,128]{3,2,1,0:T(8,128)(2,1)S(1)}, u32[]{:S(2)}, u32[]{:S(2)}) collective-permute-start(bf16[2,4,128,128]{3,2,1,0:T(8,128)(2,1)S(1)} %maximum_bitcast_fusion.kv_ref), channel_id=1, source_target_pairs={{0,2},{2,4},{4,6},{1,3},{3,5},{5,7},{8,10},{10,12},{12,14},{9,11},... | collective-permute-start | bytes 786440 | tf_op jit(solution)/shard_map/ppermute | solution.py:331
  6.7 3.3 %collective-permute-start.2 = (bf16[2,4,128,128]{3,2,1,0:T(8,128)(2,1)S(1)}, bf16[2,4,128,128]{3,2,1,0:T(8,128)(2,1)S(1)}, u32[]{:S(2)}, u32[]{:S(2)}) collective-permute-start(bf16[2,4,128,128]{3,2,1,0:T(8,128)(2,1)S(1)} %maximum_bitcast_fusion.kv_ref), channel_id=1, source_target_pairs={{0,6},{1,7},{8,14},{9,15},{16,22},{17,23},{24,30},{25,31}} | collective-permute-start | bytes 786440 | tf_op jit(solution)/shard_map/ppermute | solution.py:331
  10.0 3.3 %collective-permute-done.kv_ref.refs_0_ = bf16[2,4,128,128]{3,2,1,0:T(8,128)(2,1)S(1)} collective-permute-done((bf16[2,4,128,128]{3,2,1,0:T(8,128)(2,1)S(1)}, bf16[2,4,128,128]{3,2,1,0:T(8,128)(2,1)S(1)}, u32[]{:S(2)}, u32[]{:S(2)}) %collective-permute-start) | collective-permute-done | bytes 262176 | tf_op jit(solution)/shard_map/ppermute | solution.py:331
  13.3 0.7 %collective-permute-start.1 = (bf16[2,4,128,128]{3,2,1,0:T(8,128)(2,1)S(1)}, bf16[2,4,128,128]{3,2,1,0:T(8,128)(2,1)S(1)}, u32[]{:S(2)}, u32[]{:S(2)}) collective-permute-start(bf16[2,4,128,128]{3,2,1,0:T(8,128)(2,1)S(1)} %collective-permute-done.kv_ref.refs_0_), channel_id=1, source_target_pairs={{2,4},{4,6},{3,5},{5,7},{10,12},{12,14},{11,13},{13,15},{18,20},{2... | collective-permute-start | bytes 786440 | tf_op jit(solution)/shard_map/ppermute | solution.py:331
  14.0 0.8 %bitcast_bitcast_fusion = f32[4,2,16,128]{3,2,1,0:T(8,128)S(1)} fusion(f32[1,16,512]{2,1,0:T(8,128)} %param.11, f32[1,16,512]{2,1,0:T(8,128)} %param.12), kind=kLoop, calls=%fused_computation.5 | loop fusion | flops 16384 | bytes 131072 | tf_op jit(solution)/shard_map/transpose | solution.py:337
  14.8 17.7 %all_to_all.5.raw_ref = f32[4,2,16,128]{3,2,1,0:T(8,128)S(1)} all-to-all(f32[4,2,16,128]{3,2,1,0:T(8,128)S(1)} %bitcast_bitcast_fusion), channel_id=1, replica_groups=mesh['dp'=4,'ctx'=4,'tp'=2] {'ctx'}, dimensions={0} | all-to-all | bytes 131072 | tf_op jit(solution)/shard_map/all_to_all | solution.py:338
  32.5 2.5 %past_1.1 = (bf16[4,128,2048]{2,1,0:T(8,128)(2,1)S(1)}, f32[2,2,128,128]{3,2,1,0:T(8,128)S(1)}, f32[2,2,128,128]{3,2,1,0:T(8,128)S(1)}, bf16[128,64,128]{2,1,0:T...) custom-call(s32[3]{0:T(128)} %docs_hbm.1, ...), custom_call_target="tpu_custom_call" | custom-call | flops 1073741824 | bytes 4194304 | tf_op jit(solution)/shard_map/past_1/pallas_call | solution.py:200
  35.0 0.0 collective-permute-done.1.refs_4_.refs_1_
  35.0 0.3 shard_map.95
  35.3 0.7 %collective-permute-start.6 = (bf16[2,2,128,128]{3,2,1,0:T(8,128)(2,1)S(1)}, bf16[2,2,128,128]{3,2,1,0:T(8,128)(2,1)S(1)}, u32[]{:S(2)}, u32[]{:S(2)}) collective-permute-start(bf16[2,2,128,128]{3,2,1,0:T(8,128)(2,1)S(1)} %get-tuple-element.34), channel_id=1, source_target_pairs={{4,2},{6,4},{5,3},{7,5},{12,10},{14,12},{13,11},{15,13},{20,18},{2... | collective-permute-start | bytes 393224 | tf_op jit(solution)/shard_map/ppermute | solution.py:331
  36.0 0.0 collective-permute-done.2.refs_4_.refs_2_
  36.0 0.6 %shard_map.96 = (bf16[4,128,2048]{2,1,0:T(8,128)(2,1)S(1)}, bf16[2,4,128,128]{3,2,1,0:T(8,128)(2,1)S(1)}) custom-call(s32[1,2048]{1,0:T(1,128)S(1)} %get-tuple-element.20.refs_0_.start_ref, bf16[128,64,128]{2,1,0:T(8,128)(2,1)S(1)} %get-tuple-element.21.refs_1_.q_ref, bf16[128,64,128]{2,1,0:T(8,128)(2,1)S(1)} %get-tuple-element.22.refs_2_.g_ref, ...), custom_call_target="tpu_custom_call" | custom-call | flops 1073741824 | bytes 4194304 | tf_op jit(solution)/shard_map/pallas_call | solution.py:230
  36.6 1.3 %collective-permute-start.3 = (bf16[2,4,128,128]{3,2,1,0:T(8,128)(2,1)S(1)}, bf16[2,4,128,128]{3,2,1,0:T(8,128)(2,1)S(1)}, u32[]{:S(2)}, u32[]{:S(2)}) collective-permute-start(bf16[2,4,128,128]{3,2,1,0:T(8,128)(2,1)S(1)} %get-tuple-element.30), channel_id=1, source_target_pairs={{6,0},{7,1},{14,8},{15,9},{22,16},{23,17},{30,24},{31,25}} | collective-permute-start | bytes 786440 | tf_op jit(solution)/shard_map/ppermute | solution.py:331
  37.9 0.3 shard_map.94
  38.2 0.7 %collective-permute-start.4 = (bf16[2,2,128,128]{3,2,1,0:T(8,128)(2,1)S(1)}, bf16[2,2,128,128]{3,2,1,0:T(8,128)(2,1)S(1)}, u32[]{:S(2)}, u32[]{:S(2)}) collective-permute-start(bf16[2,2,128,128]{3,2,1,0:T(8,128)(2,1)S(1)} %get-tuple-element.32), channel_id=1, source_target_pairs={{4,2},{6,4},{5,3},{7,5},{12,10},{14,12},{13,11},{15,13},{20,18},{2... | collective-permute-start | bytes 393224 | tf_op jit(solution)/shard_map/ppermute | solution.py:331
  38.8 0.0 collective-permute-done.6
  38.9 1.3 %collective-permute-start.7 = (bf16[2,2,128,128]{3,2,1,0:T(8,128)(2,1)S(1)}, bf16[2,2,128,128]{3,2,1,0:T(8,128)(2,1)S(1)}, u32[]{:S(2)}, u32[]{:S(2)}) collective-permute-start(bf16[2,2,128,128]{3,2,1,0:T(8,128)(2,1)S(1)} %add_convert_fusion), channel_id=1, source_target_pairs={{2,0},{4,2},{6,4},{3,1},{5,3},{7,5},{10,8},{12,10},{14,12},{11,9},... | collective-permute-start | bytes 393224 | tf_op jit(solution)/shard_map/ppermute | solution.py:331
  40.2 0.0 collective-permute-done.4
  40.2 1.3 %collective-permute-start.5 = (bf16[2,2,128,128]{3,2,1,0:T(8,128)(2,1)S(1)}, bf16[2,2,128,128]{3,2,1,0:T(8,128)(2,1)S(1)}, u32[]{:S(2)}, u32[]{:S(2)}) collective-permute-start(bf16[2,2,128,128]{3,2,1,0:T(8,128)(2,1)S(1)} %add_convert_fusion.1), channel_id=1, source_target_pairs={{2,0},{4,2},{6,4},{3,1},{5,3},{7,5},{10,8},{12,10},{14,12},{11,9},... | collective-permute-start | bytes 393224 | tf_op jit(solution)/shard_map/ppermute | solution.py:331
  41.5 5.5 %last.1 = (bf16[128,64,128]{2,1,0:T(8,128)(2,1)}, f32[2,4,128,128]{3,2,1,0:T(8,128)S(1)}) custom-call(s32[1,2048]{1,0:T(1,128)S(1)} %get-tuple-element.20.refs_0_.start_ref, bf16[128,64,128]{2,1,0:T(8,128)(2,1)S(1)} %get-tuple-element.21.refs_1_.q_ref, bf16[128,64,128]{2,1,0:T(8,128)(2,1)S(1)} %get-tuple-element.22.refs_2_.g_ref, ...), custom_call_target="tpu_custom_call" | custom-call | flops 2147483648 | bytes 4194304 | tf_op jit(solution)/shard_map/last/pallas_call | solution.py:281
  47.0 3.0 %collective-permute-done.3.refs_1_ = bf16[2,4,128,128]{3,2,1,0:T(8,128)(2,1)S(1)} collective-permute-done((bf16[2,4,128,128]{3,2,1,0:T(8,128)(2,1)S(1)}, bf16[2,4,128,128]{3,2,1,0:T(8,128)(2,1)S(1)}, u32[]{:S(2)}, u32[]{:S(2)}) %collective-permute-start.3) | collective-permute-done | bytes 262176 | tf_op jit(solution)/shard_map/ppermute | solution.py:331
  50.0 1.3 %collective-permute-done.7.refs_3_ = bf16[2,2,128,128]{3,2,1,0:T(8,128)(2,1)S(1)} collective-permute-done((bf16[2,2,128,128]{3,2,1,0:T(8,128)(2,1)S(1)}, bf16[2,2,128,128]{3,2,1,0:T(8,128)(2,1)S(1)}, u32[]{:S(2)}, u32[]{:S(2)}) %collective-permute-start.7) | collective-permute-done | bytes 131104 | tf_op jit(solution)/shard_map/ppermute | solution.py:331
  51.4 5.3 %collective-permute-done.5.refs_2_ = bf16[2,2,128,128]{3,2,1,0:T(8,128)(2,1)S(1)} collective-permute-done((bf16[2,2,128,128]{3,2,1,0:T(8,128)(2,1)S(1)}, bf16[2,2,128,128]{3,2,1,0:T(8,128)(2,1)S(1)}, u32[]{:S(2)}, u32[]{:S(2)}) %collective-permute-start.5) | collective-permute-done | bytes 131104 | tf_op jit(solution)/shard_map/ppermute | solution.py:331
  56.7 0.8 %sum.1 = (bf16[128,4,128]{2,1,0:T(4,128)(2,1)}, bf16[128,4,128]{2,1,0:T(4,128)(2,1)}) custom-call(f32[2,4,128,128]{3,2,1,0:T(8,128)S(1)} %get-tuple-element.29.refs_0_, bf16[2,4,128,128]{3,2,1,0:T(8,128)(2,1)S(1)} %collective-permute-done.3.refs_1_, bf16[2,2,128,128]{3,2,1,0:T(8,128)(2,1)S(1)} %collective-permute-done.5.refs_2_, ...), custom_call_target="tpu_custom_call" | custom-call | tf_op jit(solution)/shard_map/sum/pallas_call | solution.py:312
  (3 shorter events, 0.1 us)
Async XLA Ops:
  1.7 11.6 %collective-permute-start = (bf16[2,4,128,128]{3,2,1,0:T(8,128)(2,1)S(1)}, bf16[2,4,128,128]{3,2,1,0:T(8,128)(2,1)S(1)}, u32[]{:S(2)}, u32[]{:S(2)}) collective-permute-start(bf16[2,4,128,128]{3,2,1,0:T(8,128)(2,1)S(1)} %maximum_bitcast_fusion.kv_ref), channel_id=1, source_target_pairs={{0,2},{2,4},{4,6},{1,3},{3,5},{5,7},{8,10},{10,12},{12,14},{9,11},... | collective-permute-start | bytes 786440 | tf_op jit(solution)/shard_map/ppermute | solution.py:331
  6.7 29.3 %collective-permute-start.2 = (bf16[2,4,128,128]{3,2,1,0:T(8,128)(2,1)S(1)}, bf16[2,4,128,128]{3,2,1,0:T(8,128)(2,1)S(1)}, u32[]{:S(2)}, u32[]{:S(2)}) collective-permute-start(bf16[2,4,128,128]{3,2,1,0:T(8,128)(2,1)S(1)} %maximum_bitcast_fusion.kv_ref), channel_id=1, source_target_pairs={{0,6},{1,7},{8,14},{9,15},{16,22},{17,23},{24,30},{25,31}} | collective-permute-start | bytes 786440 | tf_op jit(solution)/shard_map/ppermute | solution.py:331
  13.3 21.6 %collective-permute-start.1 = (bf16[2,4,128,128]{3,2,1,0:T(8,128)(2,1)S(1)}, bf16[2,4,128,128]{3,2,1,0:T(8,128)(2,1)S(1)}, u32[]{:S(2)}, u32[]{:S(2)}) collective-permute-start(bf16[2,4,128,128]{3,2,1,0:T(8,128)(2,1)S(1)} %collective-permute-done.kv_ref.refs_0_), channel_id=1, source_target_pairs={{2,4},{4,6},{3,5},{5,7},{10,12},{12,14},{11,13},{13,15},{18,20},{2... | collective-permute-start | bytes 786440 | tf_op jit(solution)/shard_map/ppermute | solution.py:331
  35.3 3.6 %collective-permute-start.6 = (bf16[2,2,128,128]{3,2,1,0:T(8,128)(2,1)S(1)}, bf16[2,2,128,128]{3,2,1,0:T(8,128)(2,1)S(1)}, u32[]{:S(2)}, u32[]{:S(2)}) collective-permute-start(bf16[2,2,128,128]{3,2,1,0:T(8,128)(2,1)S(1)} %get-tuple-element.34), channel_id=1, source_target_pairs={{4,2},{6,4},{5,3},{7,5},{12,10},{14,12},{13,11},{15,13},{20,18},{2... | collective-permute-start | bytes 393224 | tf_op jit(solution)/shard_map/ppermute | solution.py:331
  36.6 13.5 %collective-permute-start.3 = (bf16[2,4,128,128]{3,2,1,0:T(8,128)(2,1)S(1)}, bf16[2,4,128,128]{3,2,1,0:T(8,128)(2,1)S(1)}, u32[]{:S(2)}, u32[]{:S(2)}) collective-permute-start(bf16[2,4,128,128]{3,2,1,0:T(8,128)(2,1)S(1)} %get-tuple-element.30), channel_id=1, source_target_pairs={{6,0},{7,1},{14,8},{15,9},{22,16},{23,17},{30,24},{31,25}} | collective-permute-start | bytes 786440 | tf_op jit(solution)/shard_map/ppermute | solution.py:331
  38.2 2.0 %collective-permute-start.4 = (bf16[2,2,128,128]{3,2,1,0:T(8,128)(2,1)S(1)}, bf16[2,2,128,128]{3,2,1,0:T(8,128)(2,1)S(1)}, u32[]{:S(2)}, u32[]{:S(2)}) collective-permute-start(bf16[2,2,128,128]{3,2,1,0:T(8,128)(2,1)S(1)} %get-tuple-element.32), channel_id=1, source_target_pairs={{4,2},{6,4},{5,3},{7,5},{12,10},{14,12},{13,11},{15,13},{20,18},{2... | collective-permute-start | bytes 393224 | tf_op jit(solution)/shard_map/ppermute | solution.py:331
  38.9 12.5 %collective-permute-start.7 = (bf16[2,2,128,128]{3,2,1,0:T(8,128)(2,1)S(1)}, bf16[2,2,128,128]{3,2,1,0:T(8,128)(2,1)S(1)}, u32[]{:S(2)}, u32[]{:S(2)}) collective-permute-start(bf16[2,2,128,128]{3,2,1,0:T(8,128)(2,1)S(1)} %add_convert_fusion), channel_id=1, source_target_pairs={{2,0},{4,2},{6,4},{3,1},{5,3},{7,5},{10,8},{12,10},{14,12},{11,9},... | collective-permute-start | bytes 393224 | tf_op jit(solution)/shard_map/ppermute | solution.py:331
  40.2 16.5 %collective-permute-start.5 = (bf16[2,2,128,128]{3,2,1,0:T(8,128)(2,1)S(1)}, bf16[2,2,128,128]{3,2,1,0:T(8,128)(2,1)S(1)}, u32[]{:S(2)}, u32[]{:S(2)}) collective-permute-start(bf16[2,2,128,128]{3,2,1,0:T(8,128)(2,1)S(1)} %add_convert_fusion.1), channel_id=1, source_target_pairs={{2,0},{4,2},{6,4},{3,1},{5,3},{7,5},{10,8},{12,10},{14,12},{11,9},... | collective-permute-start | bytes 393224 | tf_op jit(solution)/shard_map/ppermute | solution.py:331
